TPU v7x, 32 devices: a whole 2x2x4 slice. The times are simulated.
32 devices in a mesh: dp: 8 (over y, x, core), shard: 4 (over z).
Axes of the slice: x: 2, y: 2, z: 4, core: 2. Of those that a mesh axis runs over, the one named last changes fastest.
Arguments:
- tokens: bfloat16 [8192, 1536], P(('dp', 'shard')), may hold values from -6 to 6
- cotangent: bfloat16 [8192, 1536], P(('dp', 'shard')), may hold values from -6 to 6
- seq_start: int32 [8192], P(('dp', 'shard')), may hold values from 0 to 192, as said below
- live_mask: int32 [8192], P(('dp', 'shard')), may hold values from 0 to 1, as said below
- input_proj: bfloat16 [2, 1536, 2048], P(None, None, 'shard'), may hold values from -0.15625 to 0.15625
- gate_blocks: bfloat16 [2, 16, 128, 128], P(None, 'shard'), may hold values from -0.5 to 0.5
- output_proj: bfloat16 [2048, 1536], P('shard'), may hold values from -0.375 to 0.375
- ffn_gate_up: bfloat16 [2, 1536, 4608], P(None, None, 'shard'), may hold values from -0.15625 to 0.15625
- ffn_down: bfloat16 [4608, 1536], P('shard'), may hold values from -0.1875 to 0.1875
- conv_taps: bfloat16 [5, 2048], P(None, 'shard'), may hold values from -3 to 3
- gate_bias: bfloat16 [2, 2048], P(None, 'shard'), may hold values from -3 to 3
- decay_param: bfloat16 [2048], P('shard'), may hold values from 3 to 8
- norm_gains: bfloat16 [2, 1536], P(None, 'shard'), may hold values from 0.5 to 1.5
- master_shard: float32 [4, 7803648], P('shard', 'dp'), may hold values from -0.75 to 0.75
- first_moment: float32 [4, 7803648], P('shard', 'dp'), may hold values from -6 to 6
- second_moment: float32 [4, 7803648], P('shard', 'dp'), may hold values from 0.1 to 10
Outputs:
- block_out: bfloat16 [8192, 1536], P(('dp', 'shard'))
- tokens_grad: bfloat16 [8192, 1536], P(('dp', 'shard'))
- weight_grads: float32 [4, 7803648], P('shard', 'dp')
- new_master: float32 [4, 7803648], P('shard', 'dp')
- new_first: float32 [4, 7803648], P('shard', 'dp')
- new_second: float32 [4, 7803648], P('shard', 'dp')
- new_weights: bfloat16 [4, 7803648], P(None, 'dp')
- bias_grad: float32 [2, 2048], P(None, 'shard')
Inputs may be any that keep to these rules, and one draw needn't show every extreme that they name: Within each device's block of 256 slots the live slots form a prefix of 2, 3 or 4 times 256 // 4 slots, and some device has all its slots live; every sequence begins at a multiple of 64, and every live sequence has 64 slots or more; seq_start is constant over a sequence and equals its first slot; the block holds one to four live sequences, and its padding forms one more sequence. `live_mask`: 1 exactly on the live prefix of each device's block.
All inputs are finite; a program needn't handle non-finite values.
Results may differ from a plain program's by a relative error of at most 0.017.
Values may be sent and summed in bfloat16 or wider, within the bound.
A program may use at most 384 MiB of HBM per device.

v0:
```python
import jax
import jax.numpy as jnp
from jax import lax
from jax.sharding import PartitionSpec as P

norm_eps = 1e-06
gate_scale = 8.0
beta_one = 0.9
beta_two = 0.95
learn_rate = 0.01
weight_decay = 0.1
adam_eps = 1e-08
corr_one = 1.0 - beta_one**10.0
corr_two = 1.0 - beta_two**10.0


def rms_scale(values, gain):
    return values * lax.rsqrt(jnp.mean(values * values, axis=-1, keepdims=True) + norm_eps) * gain


def conv_mix(signal, taps, position):
    result = taps[-1] + taps[0] * signal
    for shift_by in range(1, taps.shape[0] - 1):
        moved = jnp.pad(signal, ((shift_by, 0), (0, 0)))[:-shift_by]
        result = result + taps[shift_by] * jnp.where((position >= shift_by)[:, None], moved, 0.0)
    return result


def combine_steps(earlier, later):
    decay_first, value_first = earlier
    decay_second, value_second = later
    return (decay_first * decay_second, decay_second * value_first + value_second)


def recurrence(logits, signal, branch, bias_term, decay_term, position):
    row_count = signal.shape[0]
    recur_gate = jax.nn.sigmoid(logits[0].reshape(row_count, -1) + bias_term[0])
    input_gate = jax.nn.sigmoid(logits[1].reshape(row_count, -1) + bias_term[1])
    log_decay = -gate_scale * recur_gate * jax.nn.softplus(-decay_term)
    decay_rate = jnp.where((position > 0)[:, None], jnp.exp(log_decay), 0.0)
    drive_term = jnp.sqrt(-jnp.expm1(2.0 * log_decay)) * input_gate * signal
    states = lax.associative_scan(combine_steps, (decay_rate, drive_term), axis=0)[1]
    return states * jax.nn.gelu(branch)


def gated_gelu(ffn_pre):
    return jax.nn.gelu(ffn_pre[0]) * ffn_pre[1]


def mixer_forward(
    mix_in, input_proj, gate_blocks, output_proj, conv_taps, gate_bias, decay_param, position
):
    projected = jnp.einsum("sd,kdr->ksr", mix_in, input_proj, preferred_element_type=jnp.float32)
    conv_out, conv_pull = jax.vjp(
        lambda signal, taps: conv_mix(signal, taps, position), projected[0], conv_taps
    )
    row_count = conv_out.shape[0]
    conv_low = conv_out.astype(jnp.bfloat16).reshape(
        row_count, gate_blocks.shape[1], gate_blocks.shape[2]
    )
    gate_logits = jnp.einsum(
        "shb,khbc->kshc", conv_low, gate_blocks, preferred_element_type=jnp.float32
    )
    mixed, mix_pull = jax.vjp(
        lambda logits, signal, branch, bias_term, decay_term: recurrence(
            logits, signal, branch, bias_term, decay_term, position
        ),
        gate_logits,
        conv_out,
        projected[1],
        gate_bias,
        decay_param,
    )
    mixed_low = mixed.astype(jnp.bfloat16)
    partial_out = jnp.dot(mixed_low, output_proj, preferred_element_type=jnp.float32)
    return (partial_out, (conv_pull, conv_low, mix_pull, mixed_low))


def mixer_backward(grad_out_low, mix_in, saved, input_proj, gate_blocks, output_proj):
    conv_pull, conv_low, mix_pull, mixed_low = saved
    grad_output_proj = jnp.einsum(
        "sr,sd->rd", mixed_low, grad_out_low, preferred_element_type=jnp.float32
    )
    grad_mixed = jnp.einsum(
        "sd,rd->sr", grad_out_low, output_proj, preferred_element_type=jnp.float32
    )
    grad_logits, grad_conv_direct, grad_branch, grad_bias, grad_decay = mix_pull(grad_mixed)
    logits_low = grad_logits.astype(jnp.bfloat16)
    grad_blocks = jnp.einsum(
        "shb,kshc->khbc", conv_low, logits_low, preferred_element_type=jnp.float32
    )
    grad_conv_gates = jnp.einsum(
        "kshc,khbc->shb", logits_low, gate_blocks, preferred_element_type=jnp.float32
    )
    grad_signal, grad_taps = conv_pull(
        grad_conv_direct + grad_conv_gates.reshape(grad_conv_direct.shape)
    )
    proj_low = jnp.stack([grad_signal, grad_branch]).astype(jnp.bfloat16)
    grad_input_proj = jnp.einsum(
        "sd,ksr->kdr", mix_in, proj_low, preferred_element_type=jnp.float32
    )
    grad_mix_in = jnp.einsum(
        "ksr,kdr->sd", proj_low, input_proj, preferred_element_type=jnp.float32
    )
    return (
        grad_mix_in,
        (grad_input_proj, grad_blocks, grad_output_proj, grad_taps, grad_bias, grad_decay),
    )


def ffn_forward(ffn_in_low, ffn_gate_up, ffn_down):
    ffn_pre = jnp.einsum("sd,kdf->ksf", ffn_in_low, ffn_gate_up, preferred_element_type=jnp.float32)
    ffn_act, ffn_pull = jax.vjp(gated_gelu, ffn_pre)
    ffn_low = ffn_act.astype(jnp.bfloat16)
    partial_ffn = jnp.dot(ffn_low, ffn_down, preferred_element_type=jnp.float32)
    return (partial_ffn, (ffn_pull, ffn_low))


def ffn_backward(grad_low, ffn_in_low, saved, ffn_gate_up, ffn_down):
    ffn_pull, ffn_low = saved
    grad_down = jnp.einsum("sf,sd->fd", ffn_low, grad_low, preferred_element_type=jnp.float32)
    grad_act = jnp.einsum("sd,fd->sf", grad_low, ffn_down, preferred_element_type=jnp.float32)
    grad_pre = ffn_pull(grad_act)[0]
    pre_low = grad_pre.astype(jnp.bfloat16)
    grad_gate_up = jnp.einsum(
        "sd,ksf->kdf", ffn_in_low, pre_low, preferred_element_type=jnp.float32
    )
    grad_ffn_in = jnp.einsum(
        "ksf,kdf->sd", pre_low, ffn_gate_up, preferred_element_type=jnp.float32
    )
    return (grad_ffn_in, grad_gate_up, grad_down)


def body(
    tokens,
    cotangent,
    seq_start,
    live_mask,
    input_proj,
    gate_blocks,
    output_proj,
    ffn_gate_up,
    ffn_down,
    conv_taps,
    gate_bias,
    decay_param,
    norm_gains,
    master_shard,
    first_moment,
    second_moment,
):
    slot_count = tokens.shape[0]
    position = jnp.arange(slot_count, dtype=jnp.int32) - seq_start
    mask_rows = live_mask.astype(jnp.float32)[:, None]
    stream = tokens.astype(jnp.float32)
    grad_stream = cotangent.astype(jnp.float32) * mask_rows
    shards = (
        input_proj,
        gate_blocks,
        output_proj,
        ffn_gate_up,
        ffn_down,
        conv_taps,
        gate_bias,
        decay_param,
        norm_gains,
    )
    (
        full_in,
        full_blocks,
        full_out,
        full_up,
        full_down,
        full_taps,
        full_bias,
        full_decay,
        full_gains,
    ) = (
        lax.all_gather(shards[0], "shard", axis=2, tiled=True),
        lax.all_gather(shards[1], "shard", axis=1, tiled=True),
        lax.all_gather(shards[2], "shard", axis=0, tiled=True),
        lax.all_gather(shards[3], "shard", axis=2, tiled=True),
        lax.all_gather(shards[4], "shard", axis=0, tiled=True),
        lax.all_gather(shards[5], "shard", axis=1, tiled=True),
        lax.all_gather(shards[6], "shard", axis=1, tiled=True),
        lax.all_gather(shards[7], "shard", axis=0, tiled=True),
        lax.all_gather(shards[8], "shard", axis=1, tiled=True),
    )
    gains = full_gains.astype(jnp.float32)
    normed, norm_pull = jax.vjp(rms_scale, stream, gains[0])
    mix_in = normed.astype(jnp.bfloat16)
    mix_out, mix_saved = mixer_forward(
        mix_in,
        full_in,
        full_blocks,
        full_out,
        full_taps.astype(jnp.float32),
        full_bias.astype(jnp.float32),
        full_decay.astype(jnp.float32),
        position,
    )
    residual = stream + mix_out
    normed_two, second_pull = jax.vjp(rms_scale, residual, gains[1])
    ffn_in_low = normed_two.astype(jnp.bfloat16)
    ffn_result, ffn_saved = ffn_forward(ffn_in_low, full_up, full_down)
    block_out = (mask_rows * (residual + ffn_result)).astype(jnp.bfloat16)
    grad_ffn_in, grad_up, grad_down = ffn_backward(
        grad_stream.astype(jnp.bfloat16), ffn_in_low, ffn_saved, full_up, full_down
    )
    grad_norm_two, grad_gain_two = second_pull(grad_ffn_in)
    grad_residual = grad_stream + grad_norm_two
    grad_mix_in, mix_grads = mixer_backward(
        grad_residual.astype(jnp.bfloat16), mix_in, mix_saved, full_in, full_blocks, full_out
    )
    grad_norm_one, grad_gain_one = norm_pull(grad_mix_in)
    tokens_grad = (grad_residual + grad_norm_one).astype(jnp.bfloat16)
    grads = (
        mix_grads[0],
        mix_grads[1],
        mix_grads[2],
        grad_up,
        grad_down,
        mix_grads[3],
        mix_grads[4],
        mix_grads[5],
        jnp.stack([grad_gain_one, grad_gain_two]),
    )
    summed = (
        lax.psum_scatter(
            grads[0].astype(jnp.bfloat16), "shard", scatter_dimension=2, tiled=True
        ).astype(jnp.float32),
        lax.psum_scatter(
            grads[1].astype(jnp.bfloat16), "shard", scatter_dimension=1, tiled=True
        ).astype(jnp.float32),
        lax.psum_scatter(
            grads[2].astype(jnp.bfloat16), "shard", scatter_dimension=0, tiled=True
        ).astype(jnp.float32),
        lax.psum_scatter(
            grads[3].astype(jnp.bfloat16), "shard", scatter_dimension=2, tiled=True
        ).astype(jnp.float32),
        lax.psum_scatter(
            grads[4].astype(jnp.bfloat16), "shard", scatter_dimension=0, tiled=True
        ).astype(jnp.float32),
        lax.psum_scatter(
            grads[5].astype(jnp.bfloat16), "shard", scatter_dimension=1, tiled=True
        ).astype(jnp.float32),
        lax.psum_scatter(
            grads[6].astype(jnp.bfloat16), "shard", scatter_dimension=1, tiled=True
        ).astype(jnp.float32),
        lax.psum_scatter(
            grads[7].astype(jnp.bfloat16), "shard", scatter_dimension=0, tiled=True
        ).astype(jnp.float32),
        lax.psum_scatter(
            grads[8].astype(jnp.bfloat16), "shard", scatter_dimension=1, tiled=True
        ).astype(jnp.float32),
    )
    flat = jnp.concatenate([member.reshape(1, -1) for member in summed], axis=1)
    piece = lax.psum_scatter(flat, "dp", scatter_dimension=1, tiled=True)
    bias_total = lax.psum(summed[6], "dp")
    new_first = beta_one * first_moment + (1.0 - beta_one) * piece
    new_second = beta_two * second_moment + (1.0 - beta_two) * piece * piece
    new_master = master_shard - learn_rate * (
        new_first / corr_one / (jnp.sqrt(new_second / corr_two) + adam_eps)
        + weight_decay * master_shard
    )
    new_weights = lax.all_gather(new_master.astype(jnp.bfloat16), "shard", axis=0, tiled=True)
    return (
        block_out,
        tokens_grad,
        piece,
        new_master,
        new_first,
        new_second,
        new_weights,
        bias_total,
    )


def solution(mesh):
    placed = (
        P(("dp", "shard"), None),
        P(("dp", "shard"), None),
        P(("dp", "shard")),
        P(("dp", "shard")),
        P(None, None, "shard"),
        P(None, "shard", None, None),
        P("shard", None),
        P(None, None, "shard"),
        P("shard", None),
        P(None, "shard"),
        P(None, "shard"),
        P("shard"),
        P(None, "shard"),
        P("shard", "dp"),
        P("shard", "dp"),
        P("shard", "dp"),
    )
    return jax.shard_map(
        body,
        mesh=mesh,
        in_specs=placed,
        out_specs=(
            P(("dp", "shard"), None),
            P(("dp", "shard"), None),
            P("shard", "dp"),
            P("shard", "dp"),
            P("shard", "dp"),
            P("shard", "dp"),
            P(None, "dp"),
            P(None, "shard"),
        ),
        check_vma=False,
    )
```

profile of v0, /device:TPU:0, one launch (start us, length us, event | category | flops | bytes accessed | tf_op | source)
XLA Modules:
  0.0 3224.1 jit_solution(12165404766030103313)
XLA Ops:
  10.9 13.5 all_gather.31
  25.1 19.5 all-gather
  44.6 14.4 all_gather.34
  59.0 20.0 all_gather.30
  80.1 151.1 %all-gather.9.cloned.1.call-done = bf16[2,1536,2048]{2,1,0:T(8,128)(2,1)} async-done(((bf16[2,1536,512]{2,1,0:T(8,128)(2,1)}), bf16[2,1536,2048]{2,1,0:T(8,128)(2,1)}) %all-gather.9.cloned.1.call-update) | async-done | bytes 12582928 | tf_op jit(solution)/shard_map/all_gather | solution.py:179
  242.7 16.9 all-gather.11.cloned.1.call-done
  433.7 418.2 %all-gather.15.cloned.1.call-done = bf16[2,1536,4608]{2,1,0:T(8,128)(2,1)} async-done(((bf16[2,1536,1152]{2,1,0:T(8,128)(2,1)}), bf16[2,1536,4608]{2,1,0:T(8,128)(2,1)}) %all-gather.15.cloned.1.call-update) | async-done | bytes 28311568 | tf_op jit(solution)/shard_map/all_gather | solution.py:182
  851.9 19.1 convolution_bitcast_fusion
  870.9 224.5 %all-gather.17.cloned.1.call-done = bf16[4608,1536]{1,0:T(8,128)(2,1)} async-done(((bf16[1152,1536]{1,0:T(8,128)(2,1)}), bf16[4608,1536]{1,0:T(8,128)(2,1)}) %all-gather.17.cloned.1.call-update) | async-done | bytes 14155792 | tf_op jit(solution)/shard_map/all_gather | solution.py:183
  1095.4 14.4 multiply_bitcast_fusion
  1109.9 17.7 multiply_reduce_fusion.5
  1388.2 16.6 convert_bitcast_fusion
  1407.9 27.5 reduce-scatter.16.cloned.1.call-done
  1436.5 111.2 %reduce-scatter.18.cloned.1.call-done = bf16[512,1536]{1,0:T(8,128)(2,1)} async-done(((bf16[2048,1536]{1,0:T(8,128)(2,1)}), bf16[512,1536]{1,0:T(8,128)(2,1)}) %reduce-scatter.18.cloned.1.call-update) | async-done | bytes 1572880 | tf_op jit(solution)/shard_map/reduce_scatter | solution.py:235
  1554.4 208.2 %reduce-scatter.14.cloned.1.call-done = bf16[2,1536,512]{1,2,0:T(8,128)(2,1)} async-done(((bf16[2,1536,2048]{1,2,0:T(8,128)(2,1)}), bf16[2,1536,512]{1,2,0:T(8,128)(2,1)}) %reduce-scatter.14.cloned.1.call-update) | async-done | bytes 3145744 | tf_op jit(solution)/shard_map/reduce_scatter | solution.py:229
  1768.1 14.6 reshape.196
  1792.6 210.6 %reduce-scatter.22.cloned.1.call-done = bf16[1152,1536]{1,0:T(8,128)(2,1)} async-done(((bf16[4608,1536]{1,0:T(8,128)(2,1)}), bf16[1152,1536]{1,0:T(8,128)(2,1)}) %reduce-scatter.22.cloned.1.call-update) | async-done | bytes 3538960 | tf_op jit(solution)/shard_map/reduce_scatter | solution.py:241
  2006.2 24.6 copy.106
  2030.8 440.8 %reduce-scatter.20.cloned.1.call-done = bf16[2,1536,1152]{1,2,0:T(8,128)(2,1)} async-done(((bf16[2,1536,4608]{1,2,0:T(8,128)(2,1)}), bf16[2,1536,1152]{1,2,0:T(8,128)(2,1)}) %reduce-scatter.20.cloned.1.call-update) | async-done | bytes 7077904 | tf_op jit(solution)/shard_map/reduce_scatter | solution.py:238
  2482.6 27.7 reshape.202
  2531.2 374.5 %all-reduce.96.cloned.1.call-done = f32[1,7803648]{1,0:T(1,128)} async-done(((f32[1,7803648]{1,0:T(1,128)}), f32[1,7803648]{1,0:T(1,128)}) %all-reduce.96.cloned.1.call-update) | async-done | bytes 31214608
  2905.6 30.9 convert_bitcast_fusion.3
  2950.1 12.8 psum.7
  2962.8 241.6 %all-gather.19.cloned.1.call-done = bf16[4,1,975456]{2,1,0:T(2,128)(2,1)} async-done(((bf16[1,1,975456]{2,1,0:T(2,128)(2,1)}), bf16[4,1,975456]{2,1,0:T(2,128)(2,1)}) %all-gather.19.cloned.1.call-update) | async-done | bytes 7803664 | tf_op jit(solution)/shard_map/all_gather | solution.py:266
  (577 shorter events, 535.6 us)
Async XLA Ops:
  7.2 224.1 %all-gather.9.cloned.1.call-start = ((), (), s32[]{:S(2)}) async-start(), calls=%async_computation.8 | async-start | bytes 15728640 | tf_op jit(solution)/shard_map/all_gather | solution.py:179
  7.9 251.7 %all-gather.11.cloned.1.call-start = ((), (), s32[]{:S(2)}) async-start(), calls=%async_computation.9 | async-start | bytes 1310720 | tf_op jit(solution)/shard_map/all_gather | solution.py:180
  8.9 417.5 %all-gather.13.cloned.1.call-start = ((), (), s32[]{:S(2)}) async-start(), calls=%async_computation.10 | async-start | bytes 7864320 | tf_op jit(solution)/shard_map/all_gather | solution.py:181
  9.6 842.3 %all-gather.15.cloned.1.call-start = ((), (), s32[]{:S(2)}) async-start(), calls=%async_computation.11 | async-start | bytes 35389440 | tf_op jit(solution)/shard_map/all_gather | solution.py:182
  10.3 1085.2 %all-gather.17.cloned.1.call-start = ((), (), s32[]{:S(2)}) async-start(), calls=%async_computation.12 | async-start | bytes 17694720 | tf_op jit(solution)/shard_map/all_gather | solution.py:183
  10.8 1394.0 %reduce-scatter.28.cloned.1.call-start = ((), (), s32[]{:S(2)}) async-start(), calls=%async_computation.21 | async-start | bytes 491520
  79.9 159.9 %copy-start.119 = (pred[256]{0:T(512)(128)(4,1)}, pred[256]{0:T(512)(128)(4,1)S(1)}, u32[]{:S(2)}) copy-start(pred[256]{0:T(512)(128)(4,1)S(1)} %get-tuple-element.142) | copy-start | bytes 772
  79.9 159.9 %copy-start.121 = (pred[256]{0:T(512)(128)(4,1)}, pred[256]{0:T(512)(128)(4,1)S(1)}, u32[]{:S(2)}) copy-start(pred[256]{0:T(512)(128)(4,1)S(1)} %get-tuple-element.143) | copy-start | bytes 772
  79.9 159.9 %copy-start.123 = (pred[256]{0:T(512)(128)(4,1)}, pred[256]{0:T(512)(128)(4,1)S(1)}, u32[]{:S(2)}) copy-start(pred[256]{0:T(512)(128)(4,1)S(1)} %get-tuple-element.144) | copy-start | bytes 772
  79.9 189.0 %copy-start.126 = (pred[256]{0:T(512)(128)(4,1)}, pred[256]{0:T(512)(128)(4,1)S(1)}, u32[]{:S(2)}) copy-start(pred[256]{0:T(512)(128)(4,1)S(1)} %get-tuple-element.141) | copy-start | bytes 772
  80.0 188.9 %copy-start.85 = (f32[2048]{0:T(1024)}, f32[2048]{0:T(1024)S(1)}, u32[]{:S(2)}) copy-start(f32[2048]{0:T(1024)S(1)} %broadcast_multiply_fusion) | copy-start | bytes 24580
  80.0 188.9 %copy-start.87 = (f32[1,2048]{1,0:T(1,128)}, f32[1,2048]{1,0:T(1,128)S(1)}, u32[]{:S(2)}) copy-start(f32[1,2048]{1,0:T(1,128)S(1)} %get-tuple-element.139) | copy-start | bytes 24580
  80.0 188.9 %copy-start.89 = (f32[1,2048]{1,0:T(1,128)}, f32[1,2048]{1,0:T(1,128)S(1)}, u32[]{:S(2)}) copy-start(f32[1,2048]{1,0:T(1,128)S(1)} %get-tuple-element.140) | copy-start | bytes 24580
  80.1 159.7 %copy-start.99 = (f32[1,2048]{1,0:T(1,128)}, f32[1,2048]{1,0:T(1,128)S(1)}, u32[]{:S(2)}) copy-start(f32[1,2048]{1,0:T(1,128)S(1)} %get-tuple-element.123) | copy-start | bytes 24580
  80.1 159.7 %copy-start.101 = (f32[1,2048]{1,0:T(1,128)}, f32[1,2048]{1,0:T(1,128)S(1)}, u32[]{:S(2)}) copy-start(f32[1,2048]{1,0:T(1,128)S(1)} %get-tuple-element.124) | copy-start | bytes 24580
  1345.9 60.0 %reduce-scatter.26.cloned.1.call-start = ((), (), s32[]{:S(2)}) async-start(), calls=%async_computation.20 | async-start | bytes 655360
  1347.0 60.1 %reduce-scatter.24.cloned.1.call-start = ((), (), s32[]{:S(2)}) async-start(), calls=%async_computation.18 | async-start | bytes 40960 | tf_op jit(solution)/shard_map/reduce_scatter | solution.py:244
  1347.8 87.6 %reduce-scatter.16.cloned.1.call-start = ((), (), s32[]{:S(2)}) async-start(), calls=%async_computation.14 | async-start | bytes 1310720 | tf_op jit(solution)/shard_map/reduce_scatter | solution.py:232
  1351.5 196.2 %reduce-scatter.18.cloned.1.call-start = ((), (), s32[]{:S(2)}) async-start(), calls=%async_computation.15 | async-start | bytes 7864320 | tf_op jit(solution)/shard_map/reduce_scatter | solution.py:235
  1358.7 403.9 %reduce-scatter.14.cloned.1.call-start = ((), (), s32[]{:S(2)}) async-start(), calls=%async_computation.13 | async-start | bytes 15728640 | tf_op jit(solution)/shard_map/reduce_scatter | solution.py:229
  1366.8 636.5 %reduce-scatter.22.cloned.1.call-start = ((), (), s32[]{:S(2)}) async-start(), calls=%async_computation.17 | async-start | bytes 17694720 | tf_op jit(solution)/shard_map/reduce_scatter | solution.py:241
  1377.2 1094.4 %reduce-scatter.20.cloned.1.call-start = ((), (), s32[]{:S(2)}) async-start(), calls=%async_computation.16 | async-start | bytes 35389440 | tf_op jit(solution)/shard_map/reduce_scatter | solution.py:238
  1404.8 1500.9 %all-reduce.96.cloned.1.call-start = ((), (), s32[]{:S(2)}) async-start(), calls=%async_computation.22 | async-start | bytes 62429184
  2529.3 675.1 %all-gather.19.cloned.1.call-start = ((), (), s32[]{:S(2)}) async-start(), calls=%async_computation.19 | async-start | bytes 19509760 | tf_op jit(solution)/shard_map/all_gather | solution.py:266
  (132 other events, 1834.1 us)
Sparse Core Ops, SparseCore 0:
  9.6 221.6 all-gather.8
  233.4 26.1 all-gather.10
  261.2 114.8 all-gather.12
  377.5 474.3 all-gather.14
  853.3 242.1 all-gather.16
  1346.0 18.7 reduce-scatter.27
  1367.8 19.9 reduce-scatter.25
  1390.0 17.0 reduce-scatter.23
  1410.1 25.3 reduce-scatter.15
  1438.2 109.4 reduce-scatter.17
  1550.2 212.3 reduce-scatter.13
  1764.9 238.2 reduce-scatter.21
  2005.7 465.8 reduce-scatter.19
  2529.4 376.1 all-reduce.95
  2936.7 267.6 all-gather.18
where the time goes:
time: 3240 us; the launch traced here: 3220 us
  waiting for transfers between devices  2430 us (75%)
  local copies, waits for them, and re-layouts  407 us (13%)
  other arithmetic  144 us (4%)
  matrix products  138 us (4%)
  blocking collectives  89.4 us (3%)
    reduce_scatter x1, waiting for transfers between devices, body(): lax.psum_scatter(grads[3].astype(jnp.bfloat16), 'shard', scatter_dimensio...  441 us
    all_gather x1, waiting for transfers between devices, body(): lax.all_gather(shards[3], 'shard', axis=2, tiled=True)  418 us
    unnamed x18, waiting for transfers between devices  377 us
    all_gather x1, waiting for transfers between devices, body(): lax.all_gather(new_master.astype(jnp.bfloat16), 'shard', axis=0, tiled=True)  242 us
    all_gather x1, waiting for transfers between devices, body(): lax.all_gather(shards[4], 'shard', axis=0, tiled=True)  225 us
    reduce_scatter x1, waiting for transfers between devices, body(): lax.psum_scatter(grads[4].astype(jnp.bfloat16), 'shard', scatter_dimensio...  211 us
    reduce_scatter x1, waiting for transfers between devices, body(): lax.psum_scatter(grads[0].astype(jnp.bfloat16), 'shard', scatter_dimensio...  208 us
    all_gather x1, waiting for transfers between devices, body(): lax.all_gather(shards[0], 'shard', axis=2, tiled=True)  151 us
  transfers between devices with their start and end apart: 15, of which 12 were waited for; matrix products, arithmetic and copies ran while one was open for 10% of the time, Pallas kernels for 0%

commit v1 on v0

--- a/solution.py
+++ b/solution.py
@@ -263,7 +263,25 @@
         new_first / corr_one / (jnp.sqrt(new_second / corr_two) + adam_eps)
         + weight_decay * master_shard
     )
-    new_weights = lax.all_gather(new_master.astype(jnp.bfloat16), "shard", axis=0, tiled=True)
+    x = new_master.astype(jnp.bfloat16)
+    size, index, span = (lax.axis_size("shard"), lax.axis_index("shard"), x.shape[0])
+    right = [(i, (i + 1) % size) for i in range(size)]
+    left = [(i, (i - 1) % size) for i in range(size)]
+    whole = jnp.zeros((*x.shape[:0], size * span, *x.shape[0 + 1 :]), x.dtype)
+    whole = lax.dynamic_update_slice_in_dim(whole, x, index * span, axis=0)
+    from_left = from_right = x
+    halfway = size // 2
+    for step in range(1, halfway + 1):
+        from_left = lax.ppermute(from_left, "shard", right)
+        whole = lax.dynamic_update_slice_in_dim(
+            whole, from_left, (index - step) % size * span, axis=0
+        )
+        if step < size - halfway:
+            from_right = lax.ppermute(from_right, "shard", left)
+            whole = lax.dynamic_update_slice_in_dim(
+                whole, from_right, (index + step) % size * span, axis=0
+            )
+    new_weights = whole
     return (
         block_out,
         tokens_grad,

time: 3240 us -> 3360 us (1.037)
  local copies, waits for them, and re-layouts: 407 us -> 661 us
  waiting for transfers between devices: 2430 us -> 2270 us
    dynamic_update_slice x0 -> x4, local copies, waits for them, and re-layouts: none -> 265 us  [the longest x2 132 us: body(): lax.dynamic_update_slice_in_dim(whole, from_left, (index - step) % size *...]
    all_gather x1 -> x0, waiting for transfers between devices: 242 us -> none  [body(): lax.all_gather(new_master.astype(jnp.bfloat16), 'shard', axis=0, tiled=True)]
    ppermute x0 -> x3, waiting for transfers between devices: none -> 85.5 us  [the longest x2 85.5 us: body(): from_left = lax.ppermute(from_left, 'shard', right)]
    unnamed x297 -> x308, local copies, waits for them, and re-layouts: 88.3 us -> 71.7 us
    unnamed x18 -> x17, waiting for transfers between devices: 377 us -> 377 us
  transfers between devices with their start and end apart: 15 -> 17, of which waited for: 12 -> 12; matrix products, arithmetic and copies ran while one was open for 10% -> 16% of each run, Pallas kernels for 0% -> 0%
where the time goes in v1:
time: 3360 us; the launch traced here: 3320 us
  waiting for transfers between devices  2270 us (68%)
  local copies, waits for them, and re-layouts  661 us (20%)
  other arithmetic  143 us (4%)
  matrix products  135 us (4%)
  blocking collectives  89 us (3%)
    reduce_scatter x1, waiting for transfers between devices, body(): lax.psum_scatter(grads[3].astype(jnp.bfloat16), 'shard', scatter_dimensio...  441 us
    all_gather x1, waiting for transfers between devices, body(): lax.all_gather(shards[3], 'shard', axis=2, tiled=True)  418 us
    unnamed x17, waiting for transfers between devices  377 us
    all_gather x1, waiting for transfers between devices, body(): lax.all_gather(shards[4], 'shard', axis=0, tiled=True)  225 us
    reduce_scatter x1, waiting for transfers between devices, body(): lax.psum_scatter(grads[4].astype(jnp.bfloat16), 'shard', scatter_dimensio...  211 us
    reduce_scatter x1, waiting for transfers between devices, body(): lax.psum_scatter(grads[0].astype(jnp.bfloat16), 'shard', scatter_dimensio...  210 us
    all_gather x1, waiting for transfers between devices, body(): lax.all_gather(shards[0], 'shard', axis=2, tiled=True)  151 us
    dynamic_update_slice x2, local copies, waits for them, and re-layouts, body(): lax.dynamic_update_slice_in_dim(whole, from_left, (index - step) % size *...  132 us
  transfers between devices with their start and end apart: 17, of which 12 were waited for; matrix products, arithmetic and copies ran while one was open for 16% of the time, Pallas kernels for 0%

profile of v1, /device:TPU:0, one launch (start us, length us, event | category | flops | bytes accessed | tf_op | source)
XLA Modules:
  0.0 3324.2 jit_solution(7266421348605102012)
XLA Ops:
  25.1 19.5 all-gather
  59.0 20.0 all_gather.27
  80.1 151.2 %all-gather.7.cloned.1.call-done = bf16[2,1536,2048]{2,1,0:T(8,128)(2,1)} async-done(((bf16[2,1536,512]{2,1,0:T(8,128)(2,1)}), bf16[2,1536,2048]{2,1,0:T(8,128)(2,1)}) %all-gather.7.cloned.1.call-update) | async-done | bytes 12582928 | tf_op jit(solution)/shard_map/all_gather | solution.py:179
  242.8 16.8 all-gather.9.cloned.1.call-done
  433.6 418.2 %all-gather.13.cloned.1.call-done = bf16[2,1536,4608]{2,1,0:T(8,128)(2,1)} async-done(((bf16[2,1536,1152]{2,1,0:T(8,128)(2,1)}), bf16[2,1536,4608]{2,1,0:T(8,128)(2,1)}) %all-gather.13.cloned.1.call-update) | async-done | bytes 28311568 | tf_op jit(solution)/shard_map/all_gather | solution.py:182
  851.9 18.9 convolution_bitcast_fusion
  870.8 224.6 %all-gather.15.cloned.1.call-done = bf16[4608,1536]{1,0:T(8,128)(2,1)} async-done(((bf16[1152,1536]{1,0:T(8,128)(2,1)}), bf16[4608,1536]{1,0:T(8,128)(2,1)}) %all-gather.15.cloned.1.call-update) | async-done | bytes 14155792 | tf_op jit(solution)/shard_map/all_gather | solution.py:183
  1109.8 17.8 multiply_reduce_fusion.5
  1387.4 16.6 convert_bitcast_fusion
  1408.0 27.5 reduce-scatter.16.cloned.1.call-done
  1437.4 110.4 %reduce-scatter.18.cloned.1.call-done = bf16[512,1536]{1,0:T(8,128)(2,1)} async-done(((bf16[2048,1536]{1,0:T(8,128)(2,1)}), bf16[512,1536]{1,0:T(8,128)(2,1)}) %reduce-scatter.18.cloned.1.call-update) | async-done | bytes 1572880 | tf_op jit(solution)/shard_map/reduce_scatter | solution.py:235
  1552.9 209.9 %reduce-scatter.14.cloned.1.call-done = bf16[2,1536,512]{1,2,0:T(8,128)(2,1)} async-done(((bf16[2,1536,2048]{1,2,0:T(8,128)(2,1)}), bf16[2,1536,512]{1,2,0:T(8,128)(2,1)}) %reduce-scatter.14.cloned.1.call-update) | async-done | bytes 3145744 | tf_op jit(solution)/shard_map/reduce_scatter | solution.py:229
  1768.2 14.6 reshape.196
  1792.6 210.7 %reduce-scatter.22.cloned.1.call-done = bf16[1152,1536]{1,0:T(8,128)(2,1)} async-done(((bf16[4608,1536]{1,0:T(8,128)(2,1)}), bf16[1152,1536]{1,0:T(8,128)(2,1)}) %reduce-scatter.22.cloned.1.call-update) | async-done | bytes 3538960 | tf_op jit(solution)/shard_map/reduce_scatter | solution.py:241
  2006.3 24.6 copy.90
  2030.9 440.8 %reduce-scatter.20.cloned.1.call-done = bf16[2,1536,1152]{1,2,0:T(8,128)(2,1)} async-done(((bf16[2,1536,4608]{1,2,0:T(8,128)(2,1)}), bf16[2,1536,1152]{1,2,0:T(8,128)(2,1)}) %reduce-scatter.20.cloned.1.call-update) | async-done | bytes 7077904 | tf_op jit(solution)/shard_map/reduce_scatter | solution.py:238
  2482.7 27.7 reshape.202
  2529.0 374.5 %all-reduce.96.cloned.1.call-done = f32[1,7803648]{1,0:T(1,128)} async-done(((f32[1,7803648]{1,0:T(1,128)}), f32[1,7803648]{1,0:T(1,128)}) %all-reduce.96.cloned.1.call-update) | async-done | bytes 31214608
  2903.5 30.9 fusion.88
  2938.2 85.5 %collective-permute-done = bf16[1,975456]{1,0:T(2,128)(2,1)} collective-permute-done((bf16[1,975456]{1,0:T(2,128)(2,1)}, bf16[1,975456]{1,0:T(2,128)(2,1)}, u32[]{:S(2)}, u32[]{:S(2)}) %collective-permute-start) | collective-permute-done | bytes 1950944 | tf_op jit(solution)/shard_map/ppermute | solution.py:275
  3052.3 66.2 %dynamic_update_slice.12 = bf16[4,975456]{1,0:T(4,128)(2,1)} dynamic-update-slice(bf16[4,975456]{1,0:T(4,128)(2,1)} %broadcast_in_dim.74, bf16[1,975456]{1,0:T(2,128)(2,1)} %get-tuple-element.19, s32[]{:T(128)S(6)} %select_n.76, s32[]{:T(128)} %constant.89.clone.1) | dynamic-update-slice | bytes 3901828 | tf_op jit(solution)/shard_map/dynamic_update_slice | solution.py:271
  3118.5 66.2 %dynamic_update_slice.13 = bf16[4,975456]{1,0:T(4,128)(2,1)} dynamic-update-slice(bf16[4,975456]{1,0:T(4,128)(2,1)} %dynamic_update_slice.12, bf16[1,975456]{1,0:T(2,128)(2,1)} %collective-permute-done, s32[]{:T(128)S(6)} %select_n.78, s32[]{:T(128)} %constant.89.clone.1) | dynamic-update-slice | bytes 3901828 | tf_op jit(solution)/shard_map/dynamic_update_slice | solution.py:276
  3184.8 66.2 %dynamic_update_slice.14 = bf16[4,975456]{1,0:T(4,128)(2,1)} dynamic-update-slice(bf16[4,975456]{1,0:T(4,128)(2,1)} %dynamic_update_slice.13, bf16[1,975456]{1,0:T(2,128)(2,1)} %collective-permute-done.1, s32[]{:T(128)S(6)} %select_n.80, s32[]{:T(128)} %constant.89.clone.1) | dynamic-update-slice | bytes 3901828 | tf_op jit(solution)/shard_map/dynamic_update_slice | solution.py:281
  3251.0 66.2 %dynamic_update_slice.15 = bf16[4,975456]{1,0:T(4,128)(2,1)} dynamic-update-slice(bf16[4,975456]{1,0:T(4,128)(2,1)} %dynamic_update_slice.14, bf16[1,975456]{1,0:T(2,128)(2,1)} %collective-permute-done.2, s32[]{:T(128)S(6)} %select_n.82, s32[]{:T(128)} %constant.89.clone.1) | dynamic-update-slice | bytes 3901828 | tf_op jit(solution)/shard_map/dynamic_update_slice | solution.py:276
  (597 shorter events, 580.9 us)
Async XLA Ops:
  7.2 224.1 %all-gather.7.cloned.1.call-start = ((), (), s32[]{:S(2)}) async-start(), calls=%async_computation.8 | async-start | bytes 15728640 | tf_op jit(solution)/shard_map/all_gather | solution.py:179
  7.9 251.7 %all-gather.9.cloned.1.call-start = ((), (), s32[]{:S(2)}) async-start(), calls=%async_computation.9 | async-start | bytes 1310720 | tf_op jit(solution)/shard_map/all_gather | solution.py:180
  8.9 417.5 %all-gather.11.cloned.1.call-start = ((), (), s32[]{:S(2)}) async-start(), calls=%async_computation.10 | async-start | bytes 7864320 | tf_op jit(solution)/shard_map/all_gather | solution.py:181
  9.6 842.3 %all-gather.13.cloned.1.call-start = ((), (), s32[]{:S(2)}) async-start(), calls=%async_computation.11 | async-start | bytes 35389440 | tf_op jit(solution)/shard_map/all_gather | solution.py:182
  10.3 1085.2 %all-gather.15.cloned.1.call-start = ((), (), s32[]{:S(2)}) async-start(), calls=%async_computation.12 | async-start | bytes 17694720 | tf_op jit(solution)/shard_map/all_gather | solution.py:183
  10.8 1393.4 %reduce-scatter.28.cloned.1.call-start = ((), (), s32[]{:S(2)}) async-start(), calls=%async_computation.20 | async-start | bytes 491520
  79.9 189.0 %copy-start.130 = (pred[256]{0:T(512)(128)(4,1)}, pred[256]{0:T(512)(128)(4,1)S(1)}, u32[]{:S(2)}) copy-start(pred[256]{0:T(512)(128)(4,1)S(1)} %get-tuple-element.141) | copy-start | bytes 772
  80.0 188.9 %copy-start.89 = (f32[2048]{0:T(1024)}, f32[2048]{0:T(1024)S(1)}, u32[]{:S(2)}) copy-start(f32[2048]{0:T(1024)S(1)} %broadcast_multiply_fusion) | copy-start | bytes 24580
  80.0 188.9 %copy-start.91 = (f32[1,2048]{1,0:T(1,128)}, f32[1,2048]{1,0:T(1,128)S(1)}, u32[]{:S(2)}) copy-start(f32[1,2048]{1,0:T(1,128)S(1)} %get-tuple-element.139) | copy-start | bytes 24580
  80.0 188.9 %copy-start.93 = (f32[1,2048]{1,0:T(1,128)}, f32[1,2048]{1,0:T(1,128)S(1)}, u32[]{:S(2)}) copy-start(f32[1,2048]{1,0:T(1,128)S(1)} %get-tuple-element.140) | copy-start | bytes 24580
  1345.9 59.3 %reduce-scatter.26.cloned.1.call-start = ((), (), s32[]{:S(2)}) async-start(), calls=%async_computation.19 | async-start | bytes 655360
  1347.1 60.2 %reduce-scatter.24.cloned.1.call-start = ((), (), s32[]{:S(2)}) async-start(), calls=%async_computation.18 | async-start | bytes 40960 | tf_op jit(solution)/shard_map/reduce_scatter | solution.py:244
  1347.8 87.7 %reduce-scatter.16.cloned.1.call-start = ((), (), s32[]{:S(2)}) async-start(), calls=%async_computation.14 | async-start | bytes 1310720 | tf_op jit(solution)/shard_map/reduce_scatter | solution.py:232
  1351.5 196.3 %reduce-scatter.18.cloned.1.call-start = ((), (), s32[]{:S(2)}) async-start(), calls=%async_computation.15 | async-start | bytes 7864320 | tf_op jit(solution)/shard_map/reduce_scatter | solution.py:235
  1358.7 404.0 %reduce-scatter.14.cloned.1.call-start = ((), (), s32[]{:S(2)}) async-start(), calls=%async_computation.13 | async-start | bytes 15728640 | tf_op jit(solution)/shard_map/reduce_scatter | solution.py:229
  1366.8 636.6 %reduce-scatter.22.cloned.1.call-start = ((), (), s32[]{:S(2)}) async-start(), calls=%async_computation.17 | async-start | bytes 17694720 | tf_op jit(solution)/shard_map/reduce_scatter | solution.py:241
  1376.4 1095.3 %reduce-scatter.20.cloned.1.call-start = ((), (), s32[]{:S(2)}) async-start(), calls=%async_computation.16 | async-start | bytes 35389440 | tf_op jit(solution)/shard_map/reduce_scatter | solution.py:238
  1404.1 1499.4 %all-reduce.96.cloned.1.call-start = ((), (), s32[]{:S(2)}) async-start(), calls=%async_computation.21 | async-start | bytes 62429184
  2529.0 494.8 %copy-start.121 = (f32[256]{0:T(256)S(1)}, f32[256]{0:T(256)}, u32[]{:S(2)}) copy-start(f32[256]{0:T(256)} %copy-done.120) | copy-start | bytes 3076
  2529.0 494.8 %copy-start.12 = (f32[256,1536]{1,0:T(8,128)S(1)}, f32[256,1536]{1,0:T(8,128)}, u32[]{:S(2)}) copy-start(f32[256,1536]{1,0:T(8,128)} %copy-done.11) | copy-start | bytes 4718596
  2529.0 494.8 %copy-start.15 = (bf16[256,1536]{1,0:T(8,128)(2,1)S(1)}, bf16[256,1536]{1,0:T(8,128)(2,1)}, u32[]{:S(2)}) copy-start(bf16[256,1536]{1,0:T(8,128)(2,1)} %param.16) | copy-start | bytes 2359300
  2934.4 89.3 %collective-permute-start = (bf16[1,975456]{1,0:T(2,128)(2,1)}, bf16[1,975456]{1,0:T(2,128)(2,1)}, u32[]{:S(2)}, u32[]{:S(2)}) collective-permute-start(bf16[1,975456]{1,0:T(2,128)(2,1)} %get-tuple-element.19), channel_id=1, source_target_pairs={{0,1},{1,2},{2,3},{3,0},{4,5},{5,6},{6,7},{7,4},{8,9},{9,10},{10,1... | collective-permute-start | bytes 5852744 | tf_op jit(solution)/shard_map/ppermute | solution.py:275
  2935.9 248.8 %collective-permute-start.1 = (bf16[1,975456]{1,0:T(2,128)(2,1)}, bf16[1,975456]{1,0:T(2,128)(2,1)}, u32[]{:S(2)}, u32[]{:S(2)}) collective-permute-start(bf16[1,975456]{1,0:T(2,128)(2,1)} %get-tuple-element.19), channel_id=1, source_target_pairs={{0,3},{1,0},{2,1},{3,2},{4,7},{5,4},{6,5},{7,6},{8,11},{9,8},{10,9... | collective-permute-start | bytes 5852744 | tf_op jit(solution)/shard_map/ppermute | solution.py:280
  3023.7 227.2 %collective-permute-start.2 = (bf16[1,975456]{1,0:T(2,128)(2,1)}, bf16[1,975456]{1,0:T(2,128)(2,1)}, u32[]{:S(2)}, u32[]{:S(2)}) collective-permute-start(bf16[1,975456]{1,0:T(2,128)(2,1)} %collective-permute-done), channel_id=1, source_target_pairs={{0,1},{1,2},{2,3},{3,0},{4,5},{5,6},{6,7},{7,4},{8,9},{9,10},{10,1... | collective-permute-start | bytes 5852744 | tf_op jit(solution)/shard_map/ppermute | solution.py:275
  (140 other events, 2706.4 us)
Sparse Core Ops, SparseCore 0:
  9.6 221.6 all-gather.6
  233.4 26.1 all-gather.8
  261.2 114.8 all-gather.10
  377.5 474.3 all-gather.12
  853.3 242.0 all-gather.14
  1346.1 18.7 reduce-scatter.27
  1367.8 20.0 reduce-scatter.25
  1390.2 17.0 reduce-scatter.23
  1410.2 25.3 reduce-scatter.15
  1438.4 109.3 reduce-scatter.17
  1550.3 212.3 reduce-scatter.13
  1765.0 238.2 reduce-scatter.21
  2005.8 465.8 reduce-scatter.19
  2527.3 376.1 all-reduce.95
